TPU v7x, 32 devices: a whole 2x2x4 slice. The times are simulated.
32 devices in a mesh: layout: 4 (over z), gx: 4 (over y, core), gy: 2 (over x).
Axes of the slice: x: 2, y: 2, z: 4, core: 2. Of those that a mesh axis runs over, the one named last changes fastest.
Arguments:
- state: float32 [4, 4, 64, 32, 256], P('layout', None, 'gx', None, 'gy'), may hold values from -2 to 2
- planes: float32 [8, 4, 32, 256], P('layout', None, None, 'gy'), may hold values from -2 to 2
- turbine_cell: int32 [4, 64, 32, 256], P('layout', 'gx', None, 'gy'), may hold values from -1 to 15, as said below
- active: int32 [4, 16], P('layout'), may hold values 0 or 1
- yaw_sector: int32 [4, 16], P('layout'), may hold values from 0 to 7
- slot: int32 [4], replicated, may hold values from 0 to 7
Outputs:
- fields: float32 [4, 4, 64, 32, 256], P('layout', None, 'gx', None, 'gy')
Inputs may be any that keep to these rules, and one draw needn't show every extreme that they name: `turbine_cell`: cells of value t form turbine t's actuator disk: one streamwise cell, 11 levels around level 16 and 11 spanwise cells (periodic). Every turbine has its disk and disks don't intersect; -1 elsewhere.
All inputs are finite; a program needn't handle non-finite values. No bound on the sum of `active` on one device may be relied on, other than what follows from the above.
Results may differ from a plain program's by a relative error of at most 0.00015.
Values sent between devices are 32-bit elements; how exact they have to be, the bound alone decides.
A program may use at most 64 MiB of HBM per device.

v0:
```python
import functools

import jax
import jax.numpy as jnp
from jax import lax
from jax.experimental import pallas as pl
from jax.experimental.pallas import tpu as pltpu
from jax.sharding import PartitionSpec as P

STEPS = 4
SWEEPS = 4
RADIUS = 5

TIME_STEP = 0.25
VISCOSITY = 0.02
SMAGORINSKY = 0.0289
DIFFUSIVITY_RATIO = 1.0 / 0.7
BUOYANCY = 0.5
THRUST_COEFF = 1.33
YAW_INCREMENT = 0.1
MESH = pl.DeviceIdType.MESH


def profiles(levels):
    height = (jnp.arange(levels).astype(jnp.float32) + 0.5) / levels
    return jnp.stack([height ** (1.0 / 7.0), 0.5 * height])


def kernel(
    NL, GX, L, R, K, H, turbines, held, columns,
    slot, table, prof, ids, state, planes,
    out,
    F, G, U, RR, PP, PL, ID, SU, FO, TS,
    e_s, e_r, i_s, i_r, p_s, p_r, a_s, a_r, b_s, b_r, c_s, c_r, t_s, t_r, o_s, o_r, loc,
):
    lay = lax.axis_index("layout")
    gx = lax.axis_index("gx")
    gy = lax.axis_index("gy")
    N = GX * L

    def turned(g, q):
        odd = lax.rem(g, 2)
        return q + odd * (L - 1 - 2 * q)

    s = gx * L + turned(gx, gy)
    first = s == 0
    last = s == N - 1

    def device_of(t):
        g = t // L
        return {"gx": g, "gy": turned(g, lax.rem(t, L))}

    right = device_of(lax.rem(s + 1, N))
    left = device_of(lax.rem(s + N - 1, N))

    barrier = pltpu.get_barrier_semaphore()
    for d in range(1, N):
        pl.semaphore_signal(barrier, inc=1, device_id=device_of(lax.rem(s + d, N)), device_id_type=MESH)

    @pl.when(gx == 0)
    def _():
        for d in range(1, NL):
            for j in range(L):
                pl.semaphore_signal(
                    barrier, inc=1,
                    device_id={"layout": lax.rem(lay + d, NL), "gx": 0, "gy": j},
                    device_id_type=MESH,
                )

    q_me = turned(gx, gy)
    own_state = pltpu.make_async_copy(
        state.at[0, :, pl.ds(q_me * R, R)], F.at[:, pl.ds(1, R), gy], loc.at[0]
    )
    own_ids = pltpu.make_async_copy(ids.at[q_me], ID.at[gy], loc.at[1])
    own_state.start()
    own_ids.start()
    own_planes = pltpu.make_async_copy(
        planes, PL.at[pl.ds(lay * held, held), :, gy], loc.at[2]
    )

    @pl.when(first)
    def _():
        own_planes.start()

    zero = jnp.zeros((L, K, 128), jnp.float32)
    for buf in [RR] + [PP.at[i] for i in range(SWEEPS)]:
        @pl.when(first)
        def _():
            def body(i, c):
                buf[i] = zero
                return c
            lax.fori_loop(0, H, body, 0)

        @pl.when(last)
        def _():
            def body(i, c):
                buf[R + H + i] = zero
                return c
            lax.fori_loop(0, H, body, 0)

    pl.semaphore_wait(barrier, N - 1 + jnp.where(gx == 0, (NL - 1) * L, 0))

    def ids_copy(d):
        peer = lax.rem(gy + d, L)
        return pltpu.make_async_remote_copy(
            src_ref=ids.at[turned(gx, peer)], dst_ref=ID.at[gy],
            send_sem=i_s.at[d], recv_sem=i_r.at[d],
            device_id={"gy": peer}, device_id_type=MESH,
        )

    def ids_landing(d):
        return pltpu.make_async_remote_copy(
            src_ref=ids.at[q_me], dst_ref=ID.at[lax.rem(gy + L - d, L)],
            send_sem=i_s.at[d], recv_sem=i_r.at[d],
            device_id={"gy": lax.rem(gy + L - d, L)}, device_id_type=MESH,
        )

    def state_copy(d):
        peer = lax.rem(gy + d, L)
        return pltpu.make_async_remote_copy(
            src_ref=state.at[0, :, pl.ds(turned(gx, peer) * R, R)],
            dst_ref=F.at[:, pl.ds(1, R), gy],
            send_sem=e_s.at[d], recv_sem=e_r.at[d],
            device_id={"gy": peer}, device_id_type=MESH,
        )

    def state_landing(d):
        peer = lax.rem(gy + L - d, L)
        return pltpu.make_async_remote_copy(
            src_ref=state.at[0, :, pl.ds(q_me * R, R)],
            dst_ref=F.at[:, pl.ds(1, R), peer],
            send_sem=e_s.at[d], recv_sem=e_r.at[d],
            device_id={"gy": peer}, device_id_type=MESH,
        )

    def planes_copy(d):
        return pltpu.make_async_remote_copy(
            src_ref=planes, dst_ref=PL.at[pl.ds(lay * held, held), :, gy],
            send_sem=p_s.at[d], recv_sem=p_r.at[d, gy],
            device_id={"layout": lax.rem(lay + d, NL), "gx": 0, "gy": 0},
            device_id_type=MESH,
        )

    def planes_landing(d, j):
        source = lax.rem(lay + NL - d, NL)
        return pltpu.make_async_remote_copy(
            src_ref=planes, dst_ref=PL.at[pl.ds(source * held, held), :, j],
            send_sem=p_s.at[d], recv_sem=p_r.at[d, j],
            device_id={"layout": source, "gx": 0, "gy": j},
            device_id_type=MESH,
        )

    for d in range(1, L):
        ids_copy(d).start()
        state_copy(d).start()

    @pl.when(gx == 0)
    def _():
        for d in range(1, NL):
            planes_copy(d).start()

        @pl.when(gy != 0)
        def _():
            planes_copy(0).start()

    own_ids.wait()
    for d in range(1, L):
        ids_copy(d).wait_send()
        ids_landing(d).wait_recv()

    lane = lax.broadcasted_iota(jnp.int32, (K, 128), 1)
    level = lax.broadcasted_iota(jnp.int32, (K, 128), 0)
    at_first, at_last = lane == 0, lane == 127
    at_floor, at_top = level == 0, level == K - 1
    low = K // 2 - RADIUS
    in_band = (level >= low) & (level <= low + 2 * RADIUS)

    def beside_y(tiles, l):
        f = tiles[l]
        before = pltpu.roll(jnp.where(at_last, tiles[(l - 1) % L], f), 1, 1)
        after = pltpu.roll(jnp.where(at_first, tiles[(l + 1) % L], f), 127, 1)
        return before, after

    def beside_k(f, keep=True):
        edge = f if keep else jnp.zeros_like(f)
        below = jnp.where(at_floor, edge, pltpu.roll(f, 1, 0))
        above = jnp.where(at_top, edge, pltpu.roll(f, K - 1, 0))
        return below, above

    ID_all = [ID[l] for l in range(L)]
    cosines = [jnp.zeros((R, 128), jnp.float32) for l in range(L)]
    sines = [jnp.zeros((R, 128), jnp.float32) for l in range(L)]
    runs = [jnp.zeros((R, 128), jnp.float32) for l in range(L)]
    for t in range(turbines):
        for l in range(L):
            here = ID_all[l] == t
            cosines[l] = jnp.where(here, table[0, t], cosines[l])
            sines[l] = jnp.where(here, table[1, t], sines[l])
            runs[l] = jnp.where(here, table[2, t], runs[l])
    for l in range(L):
        FO[2, l] = cosines[l]
        FO[3, l] = sines[l]
        FO[4, l] = runs[l]

    def disk_forces():
        lane_r = lax.broadcasted_iota(jnp.int32, (R, 128), 1)
        names = [ID[l] for l in range(L)]
        normal = [SU[0, l] * FO[2, l] + SU[1, l] * FO[3, l] for l in range(L)]
        for l in range(L):
            total = normal[l]
            for shift in range(1, 2 * RADIUS + 1):
                for towards in (-1, 1):
                    other = (l - towards) % L
                    amount = shift if towards == 1 else 128 - shift
                    wraps = (lane_r >= 128 - shift) if towards == 1 else (lane_r < shift)
                    n_sh = pltpu.roll(jnp.where(wraps, normal[other], normal[l]), amount, 1)
                    i_sh = pltpu.roll(jnp.where(wraps, names[other], names[l]), amount, 1)
                    total = total + jnp.where(i_sh == names[l], n_sh, 0.0)
            speed = total / float((2 * RADIUS + 1) ** 2)
            thrust = -0.5 * THRUST_COEFF * speed * jnp.abs(speed) * FO[4, l]
            FO[0, l] = thrust * FO[2, l]
            FO[1, l] = thrust * FO[3, l]

    def disk_sums(row, l, u, v):
        SU[0, l, pl.ds(row, 1), :] = jnp.sum(jnp.where(in_band, u, 0.0), axis=0, keepdims=True)
        SU[1, l, pl.ds(row, 1), :] = jnp.sum(jnp.where(in_band, v, 0.0), axis=0, keepdims=True)

    groups = K // 8
    width = 128 // groups
    lane_8 = lax.broadcasted_iota(jnp.int32, (8, 128), 1)

    def theta_copy(par, d):
        return pltpu.make_async_remote_copy(
            src_ref=TS.at[par, 0], dst_ref=TS.at[par, d],
            send_sem=t_s.at[par, d], recv_sem=t_r.at[par, d],
            device_id=device_of(lax.rem(s + d, N)), device_id_type=MESH,
        )

    def send_theta(par, total):
        packed = jnp.zeros((8, 128), jnp.float32)
        for g in range(groups):
            part = jnp.sum(total[g * 8:(g + 1) * 8], axis=1, keepdims=True)
            packed = jnp.where(lane_8 // width == g, part, packed)
        TS[par, 0] = packed
        for d in range(1, N):
            theta_copy(par, d).start()

    def mean_theta(par):
        for d in range(1, N):
            theta_copy(par, d).wait()
        total = TS[par, 0]
        for d in range(1, N):
            total = total + TS[par, d]
        total = total / columns
        return jnp.concatenate(
            [jnp.broadcast_to(total[:, g * width:g * width + 1], (8, 128)) for g in range(groups)], axis=0
        )

    class Both:
        def __init__(self, up_src, up_dst, down_src, down_dst, send, recv):
            self.up = pltpu.make_async_remote_copy(
                src_ref=up_src, dst_ref=up_dst, send_sem=send[0], recv_sem=recv[0],
                device_id=right, device_id_type=MESH)
            self.down = pltpu.make_async_remote_copy(
                src_ref=down_src, dst_ref=down_dst, send_sem=send[1], recv_sem=recv[1],
                device_id=left, device_id_type=MESH)

        def start(self):
            @pl.when(jnp.logical_not(last))
            def _():
                self.up.start()

            @pl.when(jnp.logical_not(first))
            def _():
                self.down.start()

        def wait(self):
            @pl.when(jnp.logical_not(last))
            def _():
                self.up.wait_send()
                self.down.wait_recv()

            @pl.when(jnp.logical_not(first))
            def _():
                self.down.wait_send()
                self.up.wait_recv()

    def pair(sems, i=None):
        return (sems.at[0], sems.at[1]) if i is None else (sems.at[i, 0], sems.at[i, 1])

    def fields_exchange():
        return Both(F.at[:, R], F.at[:, 0], F.at[:, 1], F.at[:, R + 1], pair(a_s), pair(a_r))

    def speed_exchange():
        return Both(U.at[R], U.at[0], U.at[1], U.at[R + 1], pair(b_s), pair(b_r))

    def rim_exchange(buf, h, i):
        return Both(
            buf.at[pl.ds(H + R - h, h)], buf.at[pl.ds(H - h, h)],
            buf.at[pl.ds(H, h)], buf.at[pl.ds(H + R, h)], pair(c_s, i), pair(c_r, i))

    own_state.wait()
    for d in range(1, L):
        state_copy(d).wait_send()
        state_landing(d).wait_recv()

    def start_row(row, total):
        for l in range(L):
            u = F[0, row + 1, l] + prof[0]
            v = F[1, row + 1, l]
            warm = F[3, row + 1, l] + prof[1]
            F[0, row + 1, l] = u
            F[3, row + 1, l] = warm
            disk_sums(row, l, u, v)
            total = total + warm
        return total

    total = lax.fori_loop(0, R, start_row, jnp.zeros((K, 128), jnp.float32))
    fields_exchange().start()
    send_theta(0, total)

    @pl.when(gx == 0)
    def _():
        for d in range(1, NL):
            planes_copy(d).wait_send()

        @pl.when(gy != 0)
        def _():
            planes_copy(0).wait_send()

    @pl.when(first)
    def _():
        own_planes.wait()
        for d in range(NL):
            for j in range(L):
                if d or j:
                    planes_landing(d, j).wait_recv()

    def tendency_row(row, carry):
        x = row + 1
        for l in range(L):
            cen, dx, dy, dz, lap = [], [], [], [], []
            for c in range(4):
                tiles = {i % L: F[c, x, i % L] for i in (l - 1, l, l + 1)}
                f = tiles[l]
                xm, xp = F[c, x - 1, l], F[c, x + 1, l]
                ym, yp = beside_y(tiles, l)
                km, kp = beside_k(f, c != 2)
                cen.append(f)
                dx.append(xp - xm)
                dy.append(yp - ym)
                dz.append(kp - km)
                lap.append((xp + xm) + (kp + km) + (yp + ym) - 6.0 * f)
            square = 2.0 * (dx[0] * dx[0] + dy[1] * dy[1] + dz[2] * dz[2])
            for shear in (dy[0] + dx[1], dz[0] + dx[2], dz[1] + dy[2]):
                square = square + shear * shear
            nu = VISCOSITY + (0.5 * SMAGORINSKY) * jnp.sqrt(square)
            half_u, half_v, half_w = 0.5 * cen[0], 0.5 * cen[1], 0.5 * cen[2]
            for c in range(4):
                visc = nu if c < 3 else nu * DIFFUSIVITY_RATIO
                tend = lap[c] * visc - (half_u * dx[c] + half_v * dy[c] + half_w * dz[c])
                if c < 2:
                    force = FO[c, l, pl.ds(row, 1), :]
                    tend = tend + jnp.where(in_band, jnp.broadcast_to(force, (K, 128)), 0.0)
                elif c == 2:
                    tend = tend + BUOYANCY * cen[3]
                new = cen[c] + TIME_STEP * tend
                if c == 0:
                    U[x, l] = new
                else:
                    G[c - 1, row, l] = new
        return carry

    def source_row(row, mean):
        x = row + 1
        tiles = [G[0, row, l] for l in range(L)]
        for l in range(L):
            vm, vp = beside_y(tiles, l)
            w = G[1, row, l] - (TIME_STEP * BUOYANCY) * mean
            G[1, row, l] = w
            wm, wp = beside_k(w, False)
            RR[row + H, l] = ((U[x + 1, l] - U[x - 1, l]) + (vp - vm) + (wp - wm)) * 0.5
        return mean

    def sweep_row(index, from_source, x):
        old = RR if from_source else PP.at[index - 1]
        tiles = [old[x, l] for l in range(L)]
        inside = jnp.logical_not((first & (x < H)) | (last & (x >= R + H)))
        keep = jnp.where(inside, 1.0 / 6.0, 0.0).astype(jnp.float32)
        for l in range(L):
            ym, yp = beside_y(tiles, l)
            km, kp = beside_k(tiles[l])
            around = (old[x + 1, l] + old[x - 1, l]) + (ym + yp) + (km + kp)
            if from_source:
                new = (around * (-1.0 / 6.0) - tiles[l]) * keep
            else:
                new = (around - RR[x, l]) * keep
            PP[index, x, l] = new

    def sweep(index, v):
        begin, count = H - (v - 1), R + 2 * (v - 1)

        def body(i, c):
            sweep_row(index, index == 0, begin + 2 * i)
            sweep_row(index, index == 0, begin + 2 * i + 1)
            return c

        lax.fori_loop(0, count // 2, body, 0)

    def finish_row(row, total):
        x = row + H
        p = PP.at[SWEEPS - 1]
        tiles = [p[x, l] for l in range(L)]
        for l in range(L):
            ym, yp = beside_y(tiles, l)
            km, kp = beside_k(tiles[l])
            u = U[row + 1, l] - 0.5 * (p[x + 1, l] - p[x - 1, l])
            v = G[0, row, l] - 0.5 * (yp - ym)
            F[0, row + 1, l] = u
            F[1, row + 1, l] = v
            F[2, row + 1, l] = G[1, row, l] - 0.5 * (kp - km)
            warm = G[2, row, l]
            F[3, row + 1, l] = warm
            disk_sums(row, l, u, v)
            total = total + warm
        return total

    def edge_rows(body, carry):
        return lax.fori_loop(0, 2, lambda i, c: body(i * (R - 1), c), carry)

    def inner_rows(body, carry):
        return lax.fori_loop(1, R - 1, body, carry) if R > 2 else carry

    def step(n, carry):
        par = lax.rem(n, 2)

        @pl.when(first)
        def _():
            plane = slot[n]
            for c in range(4):
                for l in range(L):
                    f = PL[plane, c, l]
                    if c in (0, 3):
                        f = f + prof[0 if c == 0 else 1]
                    F[c, 0, l] = f
                    if c == 0:
                        U[0, l] = f

        @pl.when(last)
        def _():
            for c in range(4):
                F[c, R + 1] = F[c, R]

        disk_forces()
        inner_rows(tendency_row, 0)
        fields_exchange().wait()
        edge_rows(tendency_row, 0)

        @pl.when(last)
        def _():
            U[R + 1] = U[R]

        speed_exchange().start()
        mean = mean_theta(par)
        inner_rows(source_row, mean)
        speed_exchange().wait()
        edge_rows(source_row, mean)

        rim_exchange(RR, H, 0).start()
        rim_exchange(RR, H, 0).wait()
        v = H
        used = 1
        for i in range(SWEEPS):
            if v == 0:
                h = min(H, SWEEPS + 1 - i)
                rim_exchange(PP.at[i - 1], h, used).start()
                rim_exchange(PP.at[i - 1], h, used).wait()
                used += 1
                v = h
            sweep(i, v)
            v -= 1
        if v == 0:
            rim_exchange(PP.at[SWEEPS - 1], 1, used).start()
            rim_exchange(PP.at[SWEEPS - 1], 1, used).wait()

        total = edge_rows(finish_row, jnp.zeros((K, 128), jnp.float32))

        @pl.when(n < STEPS - 1)
        def _():
            fields_exchange().start()

        total = inner_rows(finish_row, total)

        @pl.when(n < STEPS - 1)
        def _():
            send_theta(1 - par, total)

        return carry

    lax.fori_loop(0, STEPS, step, 0)

    def out_copy(d):
        peer = lax.rem(gy + d, L)
        return pltpu.make_async_remote_copy(
            src_ref=F.at[:, pl.ds(1, R), peer],
            dst_ref=out.at[0, :, pl.ds(q_me * R, R)],
            send_sem=o_s.at[d], recv_sem=o_r.at[d],
            device_id={"gy": peer}, device_id_type=MESH,
        )

    def out_landing(d):
        peer = lax.rem(gy + L - d, L)
        return pltpu.make_async_remote_copy(
            src_ref=F.at[:, pl.ds(1, R), peer],
            dst_ref=out.at[0, :, pl.ds(turned(gx, peer) * R, R)],
            send_sem=o_s.at[d], recv_sem=o_r.at[d],
            device_id={"gy": peer}, device_id_type=MESH,
        )

    for d in range(1, L):
        out_copy(d).start()
    own_out = pltpu.make_async_copy(
        F.at[:, pl.ds(1, R), gy], out.at[0, :, pl.ds(q_me * R, R)], loc.at[3]
    )
    own_out.start()
    own_out.wait()
    for d in range(1, L):
        out_copy(d).wait_send()
        out_landing(d).wait_recv()


def solution(mesh):
    NL, GX, L = mesh.shape["layout"], mesh.shape["gx"], mesh.shape["gy"]

    def local(state, planes, turbine_cell, active, yaw_sector, slot):
        rows, K, cols = state.shape[2:]
        R = rows // L
        H = min(R, SWEEPS + 1)
        N = GX * L
        turbines = active.shape[1]
        held = planes.shape[0]
        ids = turbine_cell[0, :, K // 2, :].reshape(L, R, cols)
        angle = (yaw_sector[0].astype(jnp.float32) - 3.5) * YAW_INCREMENT
        table = jnp.stack([jnp.cos(angle), jnp.sin(angle), active[0].astype(jnp.float32)])
        prof = jnp.broadcast_to(profiles(K)[:, :, None], (2, K, cols))
        smem = pl.BlockSpec(memory_space=pltpu.SMEM)
        vmem = pl.BlockSpec(memory_space=pltpu.VMEM)
        hbm = pl.BlockSpec(memory_space=pl.ANY)
        f32 = jnp.float32
        dma = pltpu.SemaphoreType.DMA
        return pl.pallas_call(
            functools.partial(
                kernel, NL, GX, L, R, K, H, turbines, held, float(rows * GX * cols * L)
            ),
            out_shape=jax.ShapeDtypeStruct(state.shape, f32),
            in_specs=[smem, smem, vmem, vmem, hbm, hbm],
            out_specs=hbm,
            scratch_shapes=[
                pltpu.VMEM((4, R + 2, L, K, cols), f32),
                pltpu.VMEM((3, R, L, K, cols), f32),
                pltpu.VMEM((R + 2, L, K, cols), f32),
                pltpu.VMEM((R + 2 * H, L, K, cols), f32),
                pltpu.VMEM((SWEEPS, R + 2 * H, L, K, cols), f32),
                pltpu.VMEM((held * NL, 4, L, K, cols), f32),
                pltpu.VMEM((L, R, cols), jnp.int32),
                pltpu.VMEM((2, L, R, cols), f32),
                pltpu.VMEM((5, L, R, cols), f32),
                pltpu.VMEM((2, N, 8, 128), f32),
                dma((L,)), dma((L,)), dma((L,)), dma((L,)),
                dma((NL,)), dma((NL, L)),
                dma((2,)), dma((2,)), dma((2,)), dma((2,)),
                dma((SWEEPS + 1, 2)), dma((SWEEPS + 1, 2)),
                dma((2, N)), dma((2, N)),
                dma((L,)), dma((L,)),
                dma((4,)),
            ],
            compiler_params=pltpu.CompilerParams(
                collective_id=0, has_side_effects=True, vmem_limit_bytes=40 * 1024 * 1024
            ),
        )(slot, table, prof, ids, state, planes)

    return jax.shard_map(
        local,
        mesh=mesh,
        in_specs=(
            P("layout", None, "gx", None, "gy"),
            P("layout", None, None, "gy"),
            P("layout", "gx", None, "gy"),
            P("layout", None),
            P("layout", None),
            P(),
        ),
        out_specs=P("layout", None, "gx", None, "gy"),
        check_vma=False,
    )
```

profile of v0, /device:TPU:1, one launch (start us, length us, event | category | flops | bytes accessed | tf_op | source)
XLA Modules:
  0.0 99.6 jit_solution(10447736336405233128)
XLA Ops:
  0.0 0.0 copy-start.3
  0.0 0.7 convert_element_type.26
  0.7 0.0 copy-done.3
  0.8 0.8 slice.3
  1.6 0.0 copy-start.2
  1.6 0.1 broadcast_in_dim.2.prof
  1.7 0.6 copy-done.2
  2.3 0.0 copy-start
  2.3 1.2 %copy-done = f32[1,4,16,32,128]{4,3,2,1,0:T(8,128)S(1)} copy-done((f32[1,4,16,32,128]{4,3,2,1,0:T(8,128)S(1)}, f32[1,4,16,32,128]{4,3,2,1,0:T(8,128)}, u32[]{:S(2)}) %copy-start) | copy-done | bytes 1048600
  3.5 0.0 copy-start.1
  3.5 0.9 copy-done.1
  4.4 94.2 %shard_map.64 = f32[1,4,16,32,128]{4,3,2,1,0:T(8,128)S(1)} custom-call(s32[4]{0:T(128)S(1)} %copy-done.2, f32[3,16]{1,0:T(4,128)S(1)} %pad_maximum_fusion.table, f32[2,32,128]{2,1,0:T(8,128)S(1)} %broadcast_in_dim.2.prof, s32[2,8,128]{2,1,0:T(8,128)S(1)} %bitcast.1, f32[1,4,16,32,128]{4,3,2,1,0:T(8,128)S(1)} %copy-done, f32[2,4,32,128]{3,2,1,0:T(8,128)S(1)} %copy-done.1), custom_call_target="tpu_custom_call" | custom-call | tf_op jit(solution)/shard_map/pallas_call | solution.py:551
  98.7 1.0 copy.8
  (4 shorter events, 0.1 us)
Async XLA Ops:
  0.0 0.7 copy-start.3
  1.6 0.7 copy-start.2
  2.3 1.2 %copy-start = (f32[1,4,16,32,128]{4,3,2,1,0:T(8,128)S(1)}, f32[1,4,16,32,128]{4,3,2,1,0:T(8,128)}, u32[]{:S(2)}) copy-start(f32[1,4,16,32,128]{4,3,2,1,0:T(8,128)} %state.1) | copy-start | bytes 3145732
  3.5 0.9 copy-start.1
where the time goes:
time: 102 us; the launch traced here: 99.6 us
  Pallas kernels  94.2 us (92%)
  local copies, waits for them, and re-layouts  4.61 us (5%)
    pallas_call x1, Pallas kernels, local(): pl.pallas_call(functools.partial(kernel, NL, GX, L, R, K, H, turbines, he...  94.2 us
    unnamed x9, local copies, waits for them, and re-layouts  3.69 us

commit v1 on v0

v1 whole, which is shorter than its diff:
```python
import functools

import jax
import jax.numpy as jnp
from jax import lax
from jax.experimental import pallas as pl
from jax.experimental.pallas import tpu as pltpu
from jax.sharding import PartitionSpec as P

STEPS = 4
SWEEPS = 4
RADIUS = 5

TIME_STEP = 0.25
VISCOSITY = 0.02
SMAGORINSKY = 0.0289
DIFFUSIVITY_RATIO = 1.0 / 0.7
BUOYANCY = 0.5
THRUST_COEFF = 1.33
YAW_INCREMENT = 0.1
MESH = pl.DeviceIdType.MESH


def profiles(levels):
    height = (jnp.arange(levels).astype(jnp.float32) + 0.5) / levels
    return jnp.stack([height ** (1.0 / 7.0), 0.5 * height])


def kernel(
    NL, GX, L, R, K, H, turbines, held, columns,
    slot, table, prof, ids, state, planes,
    out,
    F, G, U, RR, PP, PL, ID, SU, NM, FO, TS, EA, EM, EB, EC, EL,
    i_s, i_r, p_s, p_r, a_s, a_r, b_s, b_r, c_s, c_r, t_s, t_r, loc,
):
    lay = lax.axis_index("layout")
    gx = lax.axis_index("gx")
    gy = lax.axis_index("gy")
    N = GX * L
    s = gx * L + gy
    first = gx == 0
    last = gx == GX - 1
    inner_end = jnp.logical_not(last)
    inner_start = jnp.logical_not(first)
    up_x, down_x = lax.rem(gx + 1, GX), lax.rem(gx + GX - 1, GX)
    up_y, down_y = lax.rem(gy + 1, L), lax.rem(gy + L - 1, L)
    blocks = R // 8

    def device_of(t):
        return {"gx": t // L, "gy": lax.rem(t, L)}

    barrier = pltpu.get_barrier_semaphore()
    for d in range(1, N):
        pl.semaphore_signal(barrier, inc=1, device_id=device_of(lax.rem(s + d, N)), device_id_type=MESH)

    @pl.when(first)
    def _():
        for d in range(1, NL):
            pl.semaphore_signal(
                barrier, inc=1, device_id={"layout": lax.rem(lay + d, NL)}, device_id_type=MESH
            )

    own_state = pltpu.make_async_copy(state.at[0], F.at[:, pl.ds(1, R)], loc.at[0])
    own_planes = pltpu.make_async_copy(planes, PL.at[pl.ds(lay * held, held)], loc.at[1])
    own_state.start()

    @pl.when(first)
    def _():
        own_planes.start()

    zero = jnp.zeros((2, K, 128), jnp.float32)
    for buf in [RR] + [PP.at[i] for i in range(SWEEPS)]:
        @pl.when(first)
        def _():
            def body(i, c):
                buf[i] = zero
                return c
            lax.fori_loop(0, H, body, 0)

        @pl.when(last)
        def _():
            def body(i, c):
                buf[R + H + i] = zero
                return c
            lax.fori_loop(0, H, body, 0)

    EA[0] = zero[0]
    EB[0] = zero[0]
    for i in range(blocks):
        EC[i] = zero[0]
    ID[0] = ids[...]

    pl.semaphore_wait(barrier, N - 1 + jnp.where(first, NL - 1, 0))

    class Exchange:
        def __init__(self, send, recv):
            self.send, self.recv, self.items = send, recv, []

        def add(self, src, dst, device, out_if=None, in_if=None):
            i = len(self.items)
            copy = pltpu.make_async_remote_copy(
                src_ref=src, dst_ref=dst, send_sem=self.send.at[i], recv_sem=self.recv.at[i],
                device_id=device, device_id_type=MESH)
            self.items.append((copy, out_if, in_if))
            return self

        def rows(self, up_src, up_dst, down_src, down_dst):
            self.add(up_src, up_dst, {"gx": up_x}, inner_end, inner_start)
            return self.add(down_src, down_dst, {"gx": down_x}, inner_start, inner_end)

        def span(self, src, dst_above, dst_below):
            self.add(src, dst_above, {"gy": up_y})
            return self.add(src, dst_below, {"gy": down_y})

        def start(self, which=slice(None)):
            for copy, out_if, _ in self.items[which]:
                if out_if is None:
                    copy.start()
                else:
                    pl.when(out_if)(copy.start)

        def wait(self):
            for copy, out_if, in_if in self.items:
                if out_if is None:
                    copy.wait_send()
                    copy.wait_recv()
                else:
                    pl.when(out_if)(copy.wait_send)
                    pl.when(in_if)(copy.wait_recv)

    def ids_exchange():
        return Exchange(i_s, i_r).span(ID.at[0], ID.at[1], ID.at[2])

    def fields_exchange():
        e = Exchange(a_s, a_r).rows(F.at[:, R], F.at[:, 0], F.at[:, 1], F.at[:, R + 1])
        return e.span(EA.at[0], EA.at[1], EA.at[2]).span(NM.at[0], NM.at[1], NM.at[2])

    def speed_exchange():
        e = Exchange(b_s, b_r).rows(U.at[R], U.at[0], U.at[1], U.at[R + 1])
        return e.span(EB.at[0], EB.at[1], EB.at[2])

    def source_exchange():
        e = Exchange(c_s, c_r).rows(
            RR.at[pl.ds(R, H), 0], RR.at[pl.ds(0, H), 0],
            RR.at[pl.ds(H, H), 0], RR.at[pl.ds(H + R, H), 0])
        e.span(EC, EL.at[0, pl.ds(1, blocks)], EL.at[1, pl.ds(1, blocks)])
        for side, to in ((0, up_y), (1, down_y)):
            e.add(EC.at[blocks - 1], EL.at[side, 0], {"gx": up_x, "gy": to}, inner_end, inner_start)
            e.add(EC.at[0], EL.at[side, blocks + 1], {"gx": down_x, "gy": to}, inner_start, inner_end)
        return e

    def planes_copy(d):
        return pltpu.make_async_remote_copy(
            src_ref=planes, dst_ref=PL.at[pl.ds(lay * held, held)],
            send_sem=p_s.at[d], recv_sem=p_r.at[d],
            device_id={"layout": lax.rem(lay + d, NL)}, device_id_type=MESH,
        )

    def planes_landing(d):
        source = lax.rem(lay + NL - d, NL)
        return pltpu.make_async_remote_copy(
            src_ref=planes, dst_ref=PL.at[pl.ds(source * held, held)],
            send_sem=p_s.at[d], recv_sem=p_r.at[d],
            device_id={"layout": source}, device_id_type=MESH,
        )

    ids_exchange().start()

    @pl.when(first)
    def _():
        for d in range(1, NL):
            planes_copy(d).start()

    lane = lax.broadcasted_iota(jnp.int32, (K, 128), 1)
    level = lax.broadcasted_iota(jnp.int32, (K, 128), 0)
    at_first, at_last = lane == 0, lane == 127
    at_floor, at_top = level == 0, level == K - 1
    low = K // 2 - RADIUS
    in_band = (level >= low) & (level <= low + 2 * RADIUS)

    def beside_y(f, rim):
        before = pltpu.roll(jnp.where(at_last, rim, f), 1, 1)
        after = pltpu.roll(jnp.where(at_first, rim, f), 127, 1)
        return before, after

    def beside_k(f, keep=True):
        edge = f if keep else jnp.zeros_like(f)
        below = jnp.where(at_floor, edge, pltpu.roll(f, 1, 0))
        above = jnp.where(at_top, edge, pltpu.roll(f, K - 1, 0))
        return below, above

    def pack(packed, f, j, width):
        return jnp.where(lane // width == j, pltpu.roll(f, width * j + width // 2, 1), packed)

    def unpack(packed, j, width):
        return pltpu.roll(packed, 128 - width // 2 - width * j, 1)

    own_ids = ID[0]
    cosines = jnp.zeros((R, 128), jnp.float32)
    sines, runs = cosines, cosines
    for t in range(turbines):
        here = own_ids == t
        cosines = jnp.where(here, table[0, t], cosines)
        sines = jnp.where(here, table[1, t], sines)
        runs = jnp.where(here, table[2, t], runs)
    FO[2] = cosines
    FO[3] = sines
    FO[4] = runs

    def disk_forces():
        lane_r = lax.broadcasted_iota(jnp.int32, (R, 128), 1)
        names = [ID[i] for i in range(3)]
        normal = [NM[i] for i in range(3)]
        total = normal[0]
        for shift in range(1, 2 * RADIUS + 1):
            for other, amount, wraps in (
                (1, shift, lane_r >= 128 - shift), (2, 128 - shift, lane_r < shift)
            ):
                n_sh = pltpu.roll(jnp.where(wraps, normal[other], normal[0]), amount, 1)
                i_sh = pltpu.roll(jnp.where(wraps, names[other], names[0]), amount, 1)
                total = total + jnp.where(i_sh == names[0], n_sh, 0.0)
        speed = total / float((2 * RADIUS + 1) ** 2)
        thrust = -0.5 * THRUST_COEFF * speed * jnp.abs(speed) * FO[4]
        FO[0] = thrust * FO[2]
        FO[1] = thrust * FO[3]

    def disk_sums(row, u, v):
        SU[0, pl.ds(row, 1), :] = jnp.sum(jnp.where(in_band, u, 0.0), axis=0, keepdims=True)
        SU[1, pl.ds(row, 1), :] = jnp.sum(jnp.where(in_band, v, 0.0), axis=0, keepdims=True)

    def send_span():
        NM[0] = SU[0] * FO[2] + SU[1] * FO[3]
        fields_exchange().start(slice(2, None))

    groups = K // 8
    width = 128 // groups
    lane_8 = lax.broadcasted_iota(jnp.int32, (8, 128), 1)

    def theta_copy(par, d):
        return pltpu.make_async_remote_copy(
            src_ref=TS.at[par, 0], dst_ref=TS.at[par, d],
            send_sem=t_s.at[par, d], recv_sem=t_r.at[par, d],
            device_id=device_of(lax.rem(s + d, N)), device_id_type=MESH,
        )

    def send_theta(par, total):
        packed = jnp.zeros((8, 128), jnp.float32)
        for g in range(groups):
            part = jnp.sum(total[g * 8:(g + 1) * 8], axis=1, keepdims=True)
            packed = jnp.where(lane_8 // width == g, part, packed)
        TS[par, 0] = packed
        for d in range(1, N):
            theta_copy(par, d).start()

    def mean_theta(par):
        for d in range(1, N):
            theta_copy(par, d).wait()
        total = TS[par, 0]
        for d in range(1, N):
            total = total + TS[par, d]
        total = total / columns
        return jnp.concatenate(
            [jnp.broadcast_to(total[:, g * width:g * width + 1], (8, 128)) for g in range(groups)], axis=0
        )

    own_state.wait()

    def start_row(row, total):
        u = F[0, row + 1] + prof[0]
        v = F[1, row + 1]
        warm = F[3, row + 1] + prof[1]
        F[0, row + 1] = u
        F[3, row + 1] = warm
        disk_sums(row, u, v)
        packed = EA[0]
        for c, f in enumerate((u, v, F[2, row + 1], warm)):
            packed = pack(packed, f, c * R + row, 2)
        EA[0] = packed
        return total + warm

    total = lax.fori_loop(0, R, start_row, jnp.zeros((K, 128), jnp.float32))
    fields_exchange().start(slice(0, 2))
    send_span()
    send_theta(0, total)
    ids_exchange().wait()

    @pl.when(first)
    def _():
        own_planes.wait()
        for d in range(1, NL):
            planes_copy(d).wait_send()
            planes_landing(d).wait_recv()

    def tendency_row(row, carry):
        x = row + 1
        rims = EM[...]
        cen, dx, dy, dz, lap = [], [], [], [], []
        for c in range(4):
            f = F[c, x]
            xm, xp = F[c, x - 1], F[c, x + 1]
            ym, yp = beside_y(f, unpack(rims, c * R + row, 2))
            km, kp = beside_k(f, c != 2)
            cen.append(f)
            dx.append(xp - xm)
            dy.append(yp - ym)
            dz.append(kp - km)
            lap.append((xp + xm) + (kp + km) + (yp + ym) - 6.0 * f)
        square = 2.0 * (dx[0] * dx[0] + dy[1] * dy[1] + dz[2] * dz[2])
        for shear in (dy[0] + dx[1], dz[0] + dx[2], dz[1] + dy[2]):
            square = square + shear * shear
        nu = VISCOSITY + (0.5 * SMAGORINSKY) * jnp.sqrt(square)
        half_u, half_v, half_w = 0.5 * cen[0], 0.5 * cen[1], 0.5 * cen[2]
        for c in range(4):
            visc = nu if c < 3 else nu * DIFFUSIVITY_RATIO
            tend = lap[c] * visc - (half_u * dx[c] + half_v * dy[c] + half_w * dz[c])
            if c < 2:
                force = FO[c, pl.ds(row, 1), :]
                tend = tend + jnp.where(in_band, jnp.broadcast_to(force, (K, 128)), 0.0)
            elif c == 2:
                tend = tend + BUOYANCY * cen[3]
            new = cen[c] + TIME_STEP * tend
            if c == 0:
                U[x] = new
            else:
                G[c - 1, row] = new
            if c == 1:
                EB[0] = pack(EB[0], new, row, 2)
        return carry

    def source_row(row, mean):
        x = row + 1
        vm, vp = beside_y(G[0, row], unpack(EM[...], row, 2))
        w = G[1, row] - (TIME_STEP * BUOYANCY) * mean
        G[1, row] = w
        wm, wp = beside_k(w, False)
        r = ((U[x + 1] - U[x - 1]) + (vp - vm) + (wp - wm)) * 0.5
        RR[row + H, 0] = r
        EC[row // 8] = pack(EC[row // 8], r, lax.rem(row, 8), 16)
        return mean

    def rim_row(x, carry):
        shifted = x - H + 8
        b = shifted // 8
        merged = jnp.where(lax.rem(lane, 16) >= 8, EL[1, b], EL[0, b])
        RR[x, 1] = unpack(merged, lax.rem(shifted, 8), 16)
        return carry

    def sweep_row(index, x):
        old = RR if index == 0 else PP.at[index - 1]
        tiles = [old[x, l] for l in range(2)]
        inside = jnp.logical_not((first & (x < H)) | (last & (x >= R + H)))
        keep = jnp.where(inside, 1.0 / 6.0, 0.0).astype(jnp.float32)
        for l in range(2):
            ym, yp = beside_y(tiles[l], tiles[1 - l])
            km, kp = beside_k(tiles[l])
            around = (old[x + 1, l] + old[x - 1, l]) + (ym + yp) + (km + kp)
            if index == 0:
                new = (around * (-1.0 / 6.0) - tiles[l]) * keep
            else:
                new = (around - RR[x, l]) * keep
            PP[index, x, l] = new

    def sweep(index, v):
        begin, count = H - (v - 1), R + 2 * (v - 1)

        def body(i, c):
            sweep_row(index, begin + 2 * i)
            sweep_row(index, begin + 2 * i + 1)
            return c

        lax.fori_loop(0, count // 2, body, 0)

    def finish_row(row, total):
        x = row + H
        p = PP.at[SWEEPS - 1]
        centre = p[x, 0]
        ym, yp = beside_y(centre, p[x, 1])
        km, kp = beside_k(centre)
        u = U[row + 1] - 0.5 * (p[x + 1, 0] - p[x - 1, 0])
        v = G[0, row] - 0.5 * (yp - ym)
        w = G[1, row] - 0.5 * (kp - km)
        warm = G[2, row]
        disk_sums(row, u, v)
        packed = EA[0]
        for c, f in enumerate((u, v, w, warm)):
            F[c, row + 1] = f
            packed = pack(packed, f, c * R + row, 2)
        EA[0] = packed
        return total + warm

    def edge_rows(body, carry):
        return lax.fori_loop(0, 2, lambda i, c: body(i * (R - 1), c), carry)

    def inner_rows(body, carry):
        return lax.fori_loop(1, R - 1, body, carry)

    odd_lane = lax.rem(lane, 2) == 1

    def step(n, carry):
        par = lax.rem(n, 2)

        @pl.when(first)
        def _():
            plane = slot[n]
            for c in range(4):
                f = PL[plane, c]
                if c in (0, 3):
                    f = f + prof[0 if c == 0 else 1]
                F[c, 0] = f
                if c == 0:
                    U[0] = f

        @pl.when(last)
        def _():
            for c in range(4):
                F[c, R + 1] = F[c, R]

        fields_exchange().wait()
        EM[...] = jnp.where(odd_lane, EA[2], EA[1])
        disk_forces()
        lax.fori_loop(0, R, tendency_row, 0)

        @pl.when(last)
        def _():
            U[R + 1] = U[R]

        speed_exchange().start()
        mean = mean_theta(par)
        speed_exchange().wait()
        EM[...] = jnp.where(odd_lane, EB[2], EB[1])
        lax.fori_loop(0, R, source_row, mean)

        source_exchange().start()
        source_exchange().wait()
        lax.fori_loop(jnp.where(first, H, 0), jnp.where(last, R + H, R + 2 * H), rim_row, 0)
        for i in range(SWEEPS):
            sweep(i, H - i)

        total = edge_rows(finish_row, jnp.zeros((K, 128), jnp.float32))

        @pl.when(n < STEPS - 1)
        def _():
            fields_exchange().start(slice(0, 2))

        total = inner_rows(finish_row, total)

        @pl.when(n < STEPS - 1)
        def _():
            send_span()
            send_theta(1 - par, total)

        return carry

    lax.fori_loop(0, STEPS, step, 0)

    own_out = pltpu.make_async_copy(F.at[:, pl.ds(1, R)], out.at[0], loc.at[2])
    own_out.start()
    own_out.wait()


def solution(mesh):
    NL, GX, L = mesh.shape["layout"], mesh.shape["gx"], mesh.shape["gy"]

    def local(state, planes, turbine_cell, active, yaw_sector, slot):
        rows, K, cols = state.shape[2:]
        R = rows
        H = SWEEPS + 1
        N = GX * L
        turbines = active.shape[1]
        held = planes.shape[0]
        ids = turbine_cell[0, :, K // 2, :]
        angle = (yaw_sector[0].astype(jnp.float32) - 3.5) * YAW_INCREMENT
        table = jnp.stack([jnp.cos(angle), jnp.sin(angle), active[0].astype(jnp.float32)])
        prof = jnp.broadcast_to(profiles(K)[:, :, None], (2, K, cols))
        smem = pl.BlockSpec(memory_space=pltpu.SMEM)
        vmem = pl.BlockSpec(memory_space=pltpu.VMEM)
        hbm = pl.BlockSpec(memory_space=pl.ANY)
        f32 = jnp.float32
        dma = pltpu.SemaphoreType.DMA
        return pl.pallas_call(
            functools.partial(
                kernel, NL, GX, L, R, K, H, turbines, held, float(rows * GX * cols * L)
            ),
            out_shape=jax.ShapeDtypeStruct(state.shape, f32),
            in_specs=[smem, smem, vmem, vmem, hbm, hbm],
            out_specs=hbm,
            scratch_shapes=[
                pltpu.VMEM((4, R + 2, K, cols), f32),
                pltpu.VMEM((3, R, K, cols), f32),
                pltpu.VMEM((R + 2, K, cols), f32),
                pltpu.VMEM((R + 2 * H, 2, K, cols), f32),
                pltpu.VMEM((SWEEPS, R + 2 * H, 2, K, cols), f32),
                pltpu.VMEM((held * NL, 4, K, cols), f32),
                pltpu.VMEM((3, R, cols), jnp.int32),
                pltpu.VMEM((2, R, cols), f32),
                pltpu.VMEM((3, R, cols), f32),
                pltpu.VMEM((5, R, cols), f32),
                pltpu.VMEM((2, N, 8, 128), f32),
                pltpu.VMEM((3, K, cols), f32),
                pltpu.VMEM((K, cols), f32),
                pltpu.VMEM((3, K, cols), f32),
                pltpu.VMEM((R // 8, K, cols), f32),
                pltpu.VMEM((2, R // 8 + 2, K, cols), f32),
                dma((2,)), dma((2,)), dma((NL,)), dma((NL,)),
                dma((6,)), dma((6,)), dma((4,)), dma((4,)), dma((8,)), dma((8,)),
                dma((2, N)), dma((2, N)),
                dma((3,)),
            ],
            compiler_params=pltpu.CompilerParams(
                collective_id=0, has_side_effects=True, vmem_limit_bytes=40 * 1024 * 1024
            ),
        )(slot, table, prof, ids, state, planes)

    return jax.shard_map(
        local,
        mesh=mesh,
        in_specs=(
            P("layout", None, "gx", None, "gy"),
            P("layout", None, None, "gy"),
            P("layout", "gx", None, "gy"),
            P("layout", None),
            P("layout", None),
            P(),
        ),
        out_specs=P("layout", None, "gx", None, "gy"),
        check_vma=False,
    )
```

time: 102 us -> 120 us (1.18); the launches traced: 99.6 us -> 120 us
  Pallas kernels: 94.2 us -> 114 us
    pallas_call x1, Pallas kernels: 94.2 us -> 114 us  [local(): pl.pallas_call(functools.partial(kernel, NL, GX, L, R, K, H, turbines, he...]
where the time goes in v1:
time: 120 us
  Pallas kernels  114 us (95%)
  local copies, waits for them, and re-layouts  4.61 us (4%)
    pallas_call x1, Pallas kernels, local(): pl.pallas_call(functools.partial(kernel, NL, GX, L, R, K, H, turbines, he...  114 us
    unnamed x9, local copies, waits for them, and re-layouts  3.69 us

profile of v1, /device:TPU:1, one launch (start us, length us, event | category | flops | bytes accessed | tf_op | source)
XLA Modules:
  0.0 119.7 jit_solution(15819369938384058055)
XLA Ops:
  0.0 0.0 copy-start.3
  0.0 0.7 convert_element_type.26
  0.7 0.0 copy-done.3
  0.8 0.8 slice.3
  1.6 0.0 copy-start.2
  1.6 0.1 broadcast_in_dim.2.prof
  1.7 0.6 copy-done.2
  2.3 0.0 copy-start
  2.3 1.2 %copy-done = f32[1,4,16,32,128]{4,3,2,1,0:T(8,128)S(1)} copy-done((f32[1,4,16,32,128]{4,3,2,1,0:T(8,128)S(1)}, f32[1,4,16,32,128]{4,3,2,1,0:T(8,128)}, u32[]{:S(2)}) %copy-start) | copy-done | bytes 1048600
  3.5 0.0 copy-start.1
  3.5 0.9 copy-done.1
  4.4 114.4 %shard_map.64 = f32[1,4,16,32,128]{4,3,2,1,0:T(8,128)S(1)} custom-call(s32[4]{0:T(128)S(1)} %copy-done.2, f32[3,16]{1,0:T(4,128)S(1)} %pad_maximum_fusion.table, f32[2,32,128]{2,1,0:T(8,128)S(1)} %broadcast_in_dim.2.prof, s32[16,128]{1,0:T(8,128)S(1)} %bitcast.3, f32[1,4,16,32,128]{4,3,2,1,0:T(8,128)S(1)} %copy-done, f32[2,4,32,128]{3,2,1,0:T(8,128)S(1)} %copy-done.1), custom_call_target="tpu_custom_call" | custom-call | tf_op jit(solution)/shard_map/pallas_call | solution.py:480
  118.8 1.0 copy.10
  (4 shorter events, 0.1 us)
Async XLA Ops:
  0.0 0.7 copy-start.3
  1.6 0.7 copy-start.2
  2.3 1.2 %copy-start = (f32[1,4,16,32,128]{4,3,2,1,0:T(8,128)S(1)}, f32[1,4,16,32,128]{4,3,2,1,0:T(8,128)}, u32[]{:S(2)}) copy-start(f32[1,4,16,32,128]{4,3,2,1,0:T(8,128)} %state.1) | copy-start | bytes 3145732
  3.5 0.9 copy-start.1

commit v2 on v1

--- a/solution.py
+++ b/solution.py
@@ -30,7 +30,7 @@
     NL, GX, L, R, K, H, turbines, held, columns,
     slot, table, prof, ids, state, planes,
     out,
-    F, G, U, RR, PP, PL, ID, SU, NM, FO, TS, EA, EM, EB, EC, EL,
+    F, G, U, RR, P0, P1, P2, P3, PL, ID, SU, NM, FO, TS, EA, EM, EB, EC, EL,
     i_s, i_r, p_s, p_r, a_s, a_r, b_s, b_r, c_s, c_r, t_s, t_r, loc,
 ):
     lay = lax.axis_index("layout")
@@ -45,6 +45,7 @@
     up_x, down_x = lax.rem(gx + 1, GX), lax.rem(gx + GX - 1, GX)
     up_y, down_y = lax.rem(gy + 1, L), lax.rem(gy + L - 1, L)
     blocks = R // 8
+    PP = [P0, P1, P2, P3]
 
     def device_of(t):
         return {"gx": t // L, "gy": lax.rem(t, L)}
@@ -69,7 +70,7 @@
         own_planes.start()
 
     zero = jnp.zeros((2, K, 128), jnp.float32)
-    for buf in [RR] + [PP.at[i] for i in range(SWEEPS)]:
+    for buf in [RR] + PP:
         @pl.when(first)
         def _():
             def body(i, c):
@@ -84,10 +85,6 @@
                 return c
             lax.fori_loop(0, H, body, 0)
 
-    EA[0] = zero[0]
-    EB[0] = zero[0]
-    for i in range(blocks):
-        EC[i] = zero[0]
     ID[0] = ids[...]
 
     pl.semaphore_wait(barrier, N - 1 + jnp.where(first, NL - 1, 0))
@@ -98,9 +95,12 @@
 
         def add(self, src, dst, device, out_if=None, in_if=None):
             i = len(self.items)
-            copy = pltpu.make_async_remote_copy(
-                src_ref=src, dst_ref=dst, send_sem=self.send.at[i], recv_sem=self.recv.at[i],
-                device_id=device, device_id_type=MESH)
+
+            def copy():
+                return pltpu.make_async_remote_copy(
+                    src_ref=src, dst_ref=dst, send_sem=self.send.at[i], recv_sem=self.recv.at[i],
+                    device_id=device, device_id_type=MESH)
+
             self.items.append((copy, out_if, in_if))
             return self
 
@@ -115,18 +115,17 @@
         def start(self, which=slice(None)):
             for copy, out_if, _ in self.items[which]:
                 if out_if is None:
-                    copy.start()
+                    copy().start()
                 else:
-                    pl.when(out_if)(copy.start)
+                    pl.when(out_if)(lambda: copy().start())
 
         def wait(self):
             for copy, out_if, in_if in self.items:
                 if out_if is None:
-                    copy.wait_send()
-                    copy.wait_recv()
+                    copy().wait()
                 else:
-                    pl.when(out_if)(copy.wait_send)
-                    pl.when(in_if)(copy.wait_recv)
+                    pl.when(out_if)(lambda: copy().wait_send())
+                    pl.when(in_if)(lambda: copy().wait_recv())
 
     def ids_exchange():
         return Exchange(i_s, i_r).span(ID.at[0], ID.at[1], ID.at[2])
@@ -174,6 +173,7 @@
     lane = lax.broadcasted_iota(jnp.int32, (K, 128), 1)
     level = lax.broadcasted_iota(jnp.int32, (K, 128), 0)
     at_first, at_last = lane == 0, lane == 127
+    odd_lane = lax.rem(lane, 2) == 1
     at_floor, at_top = level == 0, level == K - 1
     low = K // 2 - RADIUS
     in_band = (level >= low) & (level <= low + 2 * RADIUS)
@@ -225,8 +225,8 @@
         FO[1] = thrust * FO[3]
 
     def disk_sums(row, u, v):
-        SU[0, pl.ds(row, 1), :] = jnp.sum(jnp.where(in_band, u, 0.0), axis=0, keepdims=True)
-        SU[1, pl.ds(row, 1), :] = jnp.sum(jnp.where(in_band, v, 0.0), axis=0, keepdims=True)
+        SU[0, row:row + 1, :] = jnp.sum(jnp.where(in_band, u, 0.0), axis=0, keepdims=True)
+        SU[1, row:row + 1, :] = jnp.sum(jnp.where(in_band, v, 0.0), axis=0, keepdims=True)
 
     def send_span():
         NM[0] = SU[0] * FO[2] + SU[1] * FO[3]
@@ -265,20 +265,19 @@
 
     own_state.wait()
 
-    def start_row(row, total):
+    total = jnp.zeros((K, 128), jnp.float32)
+    packed = zero[0]
+    for row in range(R):
         u = F[0, row + 1] + prof[0]
         v = F[1, row + 1]
         warm = F[3, row + 1] + prof[1]
         F[0, row + 1] = u
         F[3, row + 1] = warm
         disk_sums(row, u, v)
-        packed = EA[0]
         for c, f in enumerate((u, v, F[2, row + 1], warm)):
             packed = pack(packed, f, c * R + row, 2)
-        EA[0] = packed
-        return total + warm
-
-    total = lax.fori_loop(0, R, start_row, jnp.zeros((K, 128), jnp.float32))
+        total = total + warm
+    EA[0] = packed
     fields_exchange().start(slice(0, 2))
     send_span()
     send_theta(0, total)
@@ -323,78 +322,81 @@
                 U[x] = new
             else:
                 G[c - 1, row] = new
-            if c == 1:
-                EB[0] = pack(EB[0], new, row, 2)
         return carry
 
-    def source_row(row, mean):
-        x = row + 1
-        vm, vp = beside_y(G[0, row], unpack(EM[...], row, 2))
-        w = G[1, row] - (TIME_STEP * BUOYANCY) * mean
-        G[1, row] = w
-        wm, wp = beside_k(w, False)
-        r = ((U[x + 1] - U[x - 1]) + (vp - vm) + (wp - wm)) * 0.5
-        RR[row + H, 0] = r
-        EC[row // 8] = pack(EC[row // 8], r, lax.rem(row, 8), 16)
-        return mean
-
-    def rim_row(x, carry):
-        shifted = x - H + 8
-        b = shifted // 8
-        merged = jnp.where(lax.rem(lane, 16) >= 8, EL[1, b], EL[0, b])
-        RR[x, 1] = unpack(merged, lax.rem(shifted, 8), 16)
-        return carry
-
-    def sweep_row(index, x):
-        old = RR if index == 0 else PP.at[index - 1]
-        tiles = [old[x, l] for l in range(2)]
-        inside = jnp.logical_not((first & (x < H)) | (last & (x >= R + H)))
-        keep = jnp.where(inside, 1.0 / 6.0, 0.0).astype(jnp.float32)
-        for l in range(2):
-            ym, yp = beside_y(tiles[l], tiles[1 - l])
-            km, kp = beside_k(tiles[l])
-            around = (old[x + 1, l] + old[x - 1, l]) + (ym + yp) + (km + kp)
-            if index == 0:
-                new = (around * (-1.0 / 6.0) - tiles[l]) * keep
-            else:
-                new = (around - RR[x, l]) * keep
-            PP[index, x, l] = new
+    def pack_speed():
+        packed = zero[0]
+        for row in range(R):
+            packed = pack(packed, G[0, row], row, 2)
+        EB[0] = packed
+
+    def sources(mean):
+        rims = jnp.where(odd_lane, EB[2], EB[1])
+        lift = (TIME_STEP * BUOYANCY) * mean
+        for b in range(blocks):
+            packed = zero[0]
+            for j in range(8):
+                row = 8 * b + j
+                vm, vp = beside_y(G[0, row], unpack(rims, row, 2))
+                w = G[1, row] - lift
+                G[1, row] = w
+                wm, wp = beside_k(w, False)
+                r = ((U[row + 2] - U[row]) + (vp - vm) + (wp - wm)) * 0.5
+                RR[row + H, 0] = r
+                packed = pack(packed, r, j, 16)
+            EC[b] = packed
+
+    def rims():
+        right_half = lax.rem(lane, 16) >= 8
+
+        def block(b, items):
+            merged = jnp.where(right_half, EL[1, b], EL[0, b])
+            for j in items:
+                RR[8 * (b - 1) + j + H, 1] = unpack(merged, j, 16)
+
+        pl.when(inner_start)(lambda: block(0, range(8 - H, 8)))
+        for b in range(1, blocks + 1):
+            block(b, range(8))
+        pl.when(inner_end)(lambda: block(blocks + 1, range(H)))
 
     def sweep(index, v):
-        begin, count = H - (v - 1), R + 2 * (v - 1)
-
-        def body(i, c):
-            sweep_row(index, begin + 2 * i)
-            sweep_row(index, begin + 2 * i + 1)
-            return c
-
-        lax.fori_loop(0, count // 2, body, 0)
-
-    def finish_row(row, total):
-        x = row + H
-        p = PP.at[SWEEPS - 1]
-        centre = p[x, 0]
-        ym, yp = beside_y(centre, p[x, 1])
-        km, kp = beside_k(centre)
-        u = U[row + 1] - 0.5 * (p[x + 1, 0] - p[x - 1, 0])
-        v = G[0, row] - 0.5 * (yp - ym)
-        w = G[1, row] - 0.5 * (kp - km)
-        warm = G[2, row]
-        disk_sums(row, u, v)
-        packed = EA[0]
-        for c, f in enumerate((u, v, w, warm)):
-            F[c, row + 1] = f
-            packed = pack(packed, f, c * R + row, 2)
+        old = RR if index == 0 else PP[index - 1]
+        sixth = jnp.float32(1.0 / 6.0)
+        at_start = jnp.where(first, 0.0, sixth).astype(jnp.float32)
+        at_end = jnp.where(last, 0.0, sixth).astype(jnp.float32)
+        for x in range(H - (v - 1), R + H + (v - 1)):
+            keep = at_start if x < H else at_end if x >= R + H else sixth
+            tiles = [old[x, l] for l in range(2)]
+            for l in range(2):
+                ym, yp = beside_y(tiles[l], tiles[1 - l])
+                km, kp = beside_k(tiles[l])
+                around = (old[x + 1, l] + old[x - 1, l]) + (ym + yp) + (km + kp)
+                if index == 0:
+                    new = (around * (-1.0 / 6.0) - tiles[l]) * keep
+                else:
+                    new = (around - RR[x, l]) * keep
+                PP[index][x, l] = new
+
+    def finish():
+        p = PP[SWEEPS - 1]
+        total = zero[0]
+        packed = zero[0]
+        for row in range(R):
+            x = row + H
+            centre = p[x, 0]
+            ym, yp = beside_y(centre, p[x, 1])
+            km, kp = beside_k(centre)
+            u = U[row + 1] - 0.5 * (p[x + 1, 0] - p[x - 1, 0])
+            v = G[0, row] - 0.5 * (yp - ym)
+            w = G[1, row] - 0.5 * (kp - km)
+            warm = G[2, row]
+            disk_sums(row, u, v)
+            for c, f in enumerate((u, v, w, warm)):
+                F[c, row + 1] = f
+                packed = pack(packed, f, c * R + row, 2)
+            total = total + warm
         EA[0] = packed
-        return total + warm
-
-    def edge_rows(body, carry):
-        return lax.fori_loop(0, 2, lambda i, c: body(i * (R - 1), c), carry)
-
-    def inner_rows(body, carry):
-        return lax.fori_loop(1, R - 1, body, carry)
-
-    odd_lane = lax.rem(lane, 2) == 1
+        return total
 
     def step(n, carry):
         par = lax.rem(n, 2)
@@ -418,7 +420,8 @@
         fields_exchange().wait()
         EM[...] = jnp.where(odd_lane, EA[2], EA[1])
         disk_forces()
-        lax.fori_loop(0, R, tendency_row, 0)
+        lax.fori_loop(0, R // 2, lambda i, c: tendency_row(2 * i + 1, tendency_row(2 * i, c)), 0)
+        pack_speed()
 
         @pl.when(last)
         def _():
@@ -427,25 +430,19 @@
         speed_exchange().start()
         mean = mean_theta(par)
         speed_exchange().wait()
-        EM[...] = jnp.where(odd_lane, EB[2], EB[1])
-        lax.fori_loop(0, R, source_row, mean)
+        sources(mean)
 
         source_exchange().start()
         source_exchange().wait()
-        lax.fori_loop(jnp.where(first, H, 0), jnp.where(last, R + H, R + 2 * H), rim_row, 0)
+        rims()
         for i in range(SWEEPS):
             sweep(i, H - i)
 
-        total = edge_rows(finish_row, jnp.zeros((K, 128), jnp.float32))
+        total = finish()
 
         @pl.when(n < STEPS - 1)
         def _():
             fields_exchange().start(slice(0, 2))
-
-        total = inner_rows(finish_row, total)
-
-        @pl.when(n < STEPS - 1)
-        def _():
             send_span()
             send_theta(1 - par, total)
 
@@ -489,7 +486,10 @@
                 pltpu.VMEM((3, R, K, cols), f32),
                 pltpu.VMEM((R + 2, K, cols), f32),
                 pltpu.VMEM((R + 2 * H, 2, K, cols), f32),
-                pltpu.VMEM((SWEEPS, R + 2 * H, 2, K, cols), f32),
+                pltpu.VMEM((R + 2 * H, 2, K, cols), f32),
+                pltpu.VMEM((R + 2 * H, 2, K, cols), f32),
+                pltpu.VMEM((R + 2 * H, 2, K, cols), f32),
+                pltpu.VMEM((R + 2 * H, 2, K, cols), f32),
                 pltpu.VMEM((held * NL, 4, K, cols), f32),
                 pltpu.VMEM((3, R, cols), jnp.int32),
                 pltpu.VMEM((2, R, cols), f32),

time: 120 us -> 79.9 us (0.67)
  Pallas kernels: 114 us -> 74.3 us
    pallas_call x1, Pallas kernels: 114 us -> 74.3 us  [local(): pl.pallas_call(functools.partial(kernel, NL, GX, L, R, K, H, turbines, he...]
where the time goes in v2:
time: 79.9 us; the launch traced here: 79.6 us
  Pallas kernels  74.3 us (93%)
  local copies, waits for them, and re-layouts  4.61 us (6%)
    pallas_call x1, Pallas kernels, local(): pl.pallas_call(functools.partial(kernel, NL, GX, L, R, K, H, turbines, he...  74.3 us
    unnamed x9, local copies, waits for them, and re-layouts  3.69 us

profile of v2, /device:TPU:1, one launch (start us, length us, event | category | flops | bytes accessed | tf_op | source)
XLA Modules:
  0.0 79.6 jit_solution(2939382594511710833)
XLA Ops:
  0.0 0.0 copy-start.3
  0.0 0.7 convert_element_type.26
  0.7 0.0 copy-done.3
  0.8 0.8 %slice.3 = s32[1,16,1,128]{3,2,1,0:T(1,128)S(1)} slice(s32[1,16,32,128]{3,2,1,0:T(8,128)} %param.8), slice={[0:1], [0:16], [16:17], [0:128]} | slice | bytes 16384 | tf_op jit(solution)/shard_map/slice | solution.py:468
  1.6 0.0 copy-start.2
  1.6 0.1 broadcast_in_dim.2.prof
  1.7 0.6 copy-done.2
  2.3 0.0 copy-start
  2.3 1.2 %copy-done = f32[1,4,16,32,128]{4,3,2,1,0:T(8,128)S(1)} copy-done((f32[1,4,16,32,128]{4,3,2,1,0:T(8,128)S(1)}, f32[1,4,16,32,128]{4,3,2,1,0:T(8,128)}, u32[]{:S(2)}) %copy-start) | copy-done | bytes 1048600
  3.5 0.0 copy-start.1
  3.5 0.9 %copy-done.1 = f32[2,4,32,128]{3,2,1,0:T(8,128)S(1)} copy-done((f32[2,4,32,128]{3,2,1,0:T(8,128)S(1)}, f32[2,4,32,128]{3,2,1,0:T(8,128)}, u32[]{:S(2)}) %copy-start.1) | copy-done | bytes 131096
  4.4 74.3 %shard_map.64 = f32[1,4,16,32,128]{4,3,2,1,0:T(8,128)S(1)} custom-call(s32[4]{0:T(128)S(1)} %copy-done.2, f32[3,16]{1,0:T(4,128)S(1)} %pad_maximum_fusion.table, f32[2,32,128]{2,1,0:T(8,128)S(1)} %broadcast_in_dim.2.prof, s32[16,128]{1,0:T(8,128)S(1)} %bitcast.3, f32[1,4,16,32,128]{4,3,2,1,0:T(8,128)S(1)} %copy-done, f32[2,4,32,128]{3,2,1,0:T(8,128)S(1)} %copy-done.1), custom_call_target="tpu_custom_call" | custom-call | tf_op jit(solution)/shard_map/pallas_call | solution.py:477
  78.7 1.0 %copy.10 = f32[1,4,16,32,128]{4,3,2,1,0:T(8,128)} copy(f32[1,4,16,32,128]{4,3,2,1,0:T(8,128)S(1)} %shard_map.64) | data formatting | bytes 2097152
  (4 shorter events, 0.1 us)
Async XLA Ops:
  0.0 0.7 copy-start.3
  1.6 0.7 copy-start.2
  2.3 1.2 %copy-start = (f32[1,4,16,32,128]{4,3,2,1,0:T(8,128)S(1)}, f32[1,4,16,32,128]{4,3,2,1,0:T(8,128)}, u32[]{:S(2)}) copy-start(f32[1,4,16,32,128]{4,3,2,1,0:T(8,128)} %state.1) | copy-start | bytes 3145732
  3.5 0.9 %copy-start.1 = (f32[2,4,32,128]{3,2,1,0:T(8,128)S(1)}, f32[2,4,32,128]{3,2,1,0:T(8,128)}, u32[]{:S(2)}) copy-start(f32[2,4,32,128]{3,2,1,0:T(8,128)} %planes.1) | copy-start | bytes 393220
